TPU v7x, 32 devices: a whole 2x2x4 slice. The times are simulated.
32 devices in a mesh: row: 8 (over z, x), col: 4 (over y, core).
Axes of the slice: x: 2, y: 2, z: 4, core: 2. Of those that a mesh axis runs over, the one named last changes fastest.
Arguments:
- x_window: bfloat16 [3, 2048, 512], P(None, 'row', 'col'), may hold values from -6 to 6
- y_window: float32 [3, 2048], P(None, 'row'), may hold values from -6 to 6
- block_order: int32 [3], replicated, may hold values from 0 to 2, each once
- diag_inverse: bfloat16 [3, 2048, 2048], P(None, 'row'), may hold values from -0.5 to 1.5, as said below
- panel_window: bfloat16 [3, 2048, 2048], P(None, 'row', 'col'), may hold values from -0.078125 to 0.078125
- panel_trail: bfloat16 [1024, 3, 2048], P('row', None, 'col'), may hold values from -0.078125 to 0.078125
- x_trail: bfloat16 [1024, 512], P('row', 'col'), may hold values from -6 to 6
- y_trail: float32 [1024], P('row'), may hold values from -6 to 6
Outputs:
- whitened: bfloat16 [3, 2048, 512], P(None, 'row', 'col')
- white_resp: bfloat16 [3, 2048], P(None, 'row')
- trail_rhs: float32 [1024, 512], P('row', 'col')
- trail_resp: float32 [1024], P('row')
- normal_part: float32 [512, 512], P('row')
- right_part: float32 [512], P('row')
Inputs may be any that keep to these rules, and one draw needn't show every extreme that they name: Each diag_inverse[s] is lower triangular with a positive diagonal.
All inputs are finite; a program needn't handle non-finite values.
Results may differ from a plain program's by a relative error of at most 0.014.
Values may be sent and summed in bfloat16 or wider, within the bound.
No kernel may reach another device: no remote copies, remote signals or barrier semaphores. Data moves between devices by JAX's collectives and lax.ppermute only.
A program may use at most 64 MiB of HBM per device.

v0:
```python
import jax
import jax.numpy as jnp
from jax import lax
from jax.sharding import PartitionSpec as P


def shards(
    x_window, y_window, block_order, diag_inverse, panel_window, panel_trail, x_trail, y_trail
):
    steps = x_window.shape[0]
    own_rows = x_window.shape[1]
    own_cols = x_window.shape[2]
    width = panel_window.shape[2]
    block_rows = own_rows * lax.axis_size("row")
    full_cols = own_cols * lax.axis_size("col")
    normal_rows = full_cols // lax.axis_size("row")
    col_start = lax.axis_index("col") * width
    normal_start = lax.axis_index("row") * normal_rows
    trail_rows = x_trail.shape[0]
    solved_cols = []
    solved_resp = []
    out_tiles = []
    out_resp = []
    trail_total = jnp.zeros((trail_rows, full_cols), jnp.float32)
    trail_resp_total = jnp.zeros((trail_rows,), jnp.float32)
    gram = jnp.zeros((normal_rows, full_cols), jnp.float32)
    right = jnp.zeros((normal_rows,), jnp.float32)
    for s in range(steps):
        stored = block_order[s]
        pending = lax.dynamic_index_in_dim(x_window, stored, 0, keepdims=False).astype(jnp.float32)
        pending_resp = lax.dynamic_index_in_dim(y_window, stored, 0, keepdims=False)
        if s > 0:
            first = s * (s - 1) // 2
            factors = panel_window[first : first + s]
            earlier = jnp.stack(solved_cols)
            earlier_resp = jnp.stack(solved_resp)
            update = jnp.einsum("trw,twp->rp", factors, earlier, preferred_element_type=jnp.float32)
            update_resp = jnp.einsum(
                "trw,tw->r", factors, earlier_resp, preferred_element_type=jnp.float32
            )
            pending = pending - lax.psum_scatter(update, "col", scatter_dimension=1, tiled=True)
            pending_resp = pending_resp - lax.psum(update_resp, "col")
        residual = pending.astype(jnp.bfloat16)
        resid_resp = pending_resp.astype(jnp.bfloat16)
        whole, whole_resp = (
            lax.all_gather(residual, "row", axis=0, tiled=True),
            lax.all_gather(resid_resp, "row", axis=0, tiled=True),
        )
        inverse = diag_inverse[s]
        tile = jnp.dot(inverse, whole, preferred_element_type=jnp.float32).astype(jnp.bfloat16)
        tile_resp = jnp.dot(inverse, whole_resp, preferred_element_type=jnp.float32).astype(
            jnp.bfloat16
        )
        out_tiles.append(tile)
        out_resp.append(tile_resp)
        all_rows, all_resp = (
            lax.all_gather(tile, "row", axis=0, tiled=True),
            lax.all_gather(tile_resp, "row", axis=0, tiled=True),
        )
        mine = lax.all_to_all(all_rows, "col", split_axis=0, concat_axis=1, tiled=True)
        mine_resp = lax.dynamic_slice_in_dim(all_resp, col_start, width, 0)
        solved_cols.append(mine)
        solved_resp.append(mine_resp)
        factor_rows = panel_trail[:, s, :]
        trail_total = trail_total + jnp.dot(factor_rows, mine, preferred_element_type=jnp.float32)
        trail_resp_total = trail_resp_total + jnp.dot(
            factor_rows, mine_resp, preferred_element_type=jnp.float32
        )
        slab = lax.dynamic_slice_in_dim(mine, normal_start, normal_rows, 1)
        gram = gram + lax.dot_general(
            slab, mine, (((0,), (0,)), ((), ())), preferred_element_type=jnp.float32
        )
        right = right + lax.dot_general(
            slab, mine_resp, (((0,), (0,)), ((), ())), preferred_element_type=jnp.float32
        )
    share = lax.psum_scatter(
        trail_total.astype(jnp.bfloat16), "col", scatter_dimension=1, tiled=True
    ).astype(jnp.float32)
    trail_rhs = x_trail.astype(jnp.float32) - share
    gram, right, resp_sum = lax.psum((gram, right, trail_resp_total), "col")
    trail_resp = y_trail - resp_sum
    scale = 1.0 / (steps * block_rows)
    whitened = jnp.stack(out_tiles)
    white_resp = jnp.stack(out_resp)
    return (whitened, white_resp, trail_rhs, trail_resp, gram * scale, right * scale)


def solution(mesh):
    in_specs = (
        P(None, "row", "col"),
        P(None, "row"),
        P(),
        P(None, "row", None),
        P(None, "row", "col"),
        P("row", None, "col"),
        P("row", "col"),
        P("row"),
    )
    out_specs = (
        P(None, "row", "col"),
        P(None, "row"),
        P("row", "col"),
        P("row"),
        P("row", None),
        P("row"),
    )
    return jax.shard_map(shards, mesh=mesh, in_specs=in_specs, out_specs=out_specs, check_vma=False)
```

profile of v0, /device:TPU:0, one launch (start us, length us, event | category | flops | bytes accessed | tf_op | source)
XLA Modules:
  0.0 446.1 jit_solution(9087911912187497106)
XLA Ops:
  7.2 1.4 fusion.65
  14.4 0.9 constant_dynamic-slice_fusion.3
  15.3 33.2 %all-gather = bf16[1,2048,128]{2,1,0:T(8,128)(2,1)S(1)} all-gather(bf16[1,256,128]{2,1,0:T(8,128)(2,1)S(1)} %get-tuple-element.28), channel_id=2, replica_groups=mesh['row'=8,'col'=4] {'row'}, dimensions={1}, use_global_device_ids=true | all-gather | bytes 589824 | tf_op jit(solution)/shard_map/all_gather | solution.py:46
  48.5 1.7 convolution_convert_fusion.2
  50.2 31.2 %all_gather.37 = bf16[2048,128]{0,1:T(8,128)(2,1)S(1)} all-gather(bf16[256,128]{0,1:T(8,128)(2,1)S(1)} %bitcast.162), channel_id=1, replica_groups=mesh['row'=8,'col'=4] {'row'}, dimensions={0}, use_global_device_ids=true | all-gather | bytes 589824 | tf_op jit(solution)/shard_map/all_gather | solution.py:57
  81.4 0.8 copy.47
  82.3 3.5 all-to-all-start
  85.8 20.8 %all-gather.1 = bf16[1,2048]{1,0:T(2,128)(2,1)S(1)} all-gather(bf16[1,256]{1,0:T(2,128)(2,1)S(1)} %fusion.63), channel_id=3, replica_groups=mesh['row'=8,'col'=4] {'row'}, dimensions={1}, use_global_device_ids=true | all-gather | bytes 4608 | tf_op jit(solution)/shard_map/all_gather | solution.py:47
  106.6 1.6 fusion.15
  108.3 16.3 %all-gather.2 = bf16[8,1,256]{2,1,0:T(2,128)(2,1)S(1)} all-gather(bf16[1,1,256]{2,1,0:T(2,128)(2,1)S(1)} %reshape.44), channel_id=1, replica_groups=mesh['row'=8,'col'=4] {'row'}, dimensions={0}, use_global_device_ids=true | all-gather | bytes 4608 | tf_op jit(solution)/shard_map/all_gather | solution.py:58
  124.6 0.1 dynamic_slice.43
  124.7 0.1 fusion.28
  124.9 5.7 %psum.35 = f32[256]{0:T(256)S(1)} all-reduce(f32[256]{0:T(256)S(1)} %bitcast.177), channel_id=1, replica_groups=mesh['row'=8,'col'=4] {'col'}, use_global_device_ids=true, to_apply=%region_2.3 | all-reduce | flops 256 | bytes 2048 | tf_op jit(solution)/shard_map/psum | solution.py:42
  130.5 1.1 convolution_bitcast_fusion.1
  131.7 18.3 %all-gather.3 = bf16[8,1,256]{2,1,0:T(2,128)(2,1)S(1)} all-gather(bf16[1,1,256]{2,1,0:T(2,128)(2,1)S(1)} %reshape.46), channel_id=1, replica_groups=mesh['row'=8,'col'=4] {'row'}, dimensions={0}, use_global_device_ids=true | all-gather | bytes 4608 | tf_op jit(solution)/shard_map/all_gather | solution.py:47
  150.0 1.6 fusion.12
  151.7 16.3 %all-gather.4 = bf16[8,1,256]{2,1,0:T(2,128)(2,1)S(1)} all-gather(bf16[1,1,256]{2,1,0:T(2,128)(2,1)S(1)} %reshape.48), channel_id=1, replica_groups=mesh['row'=8,'col'=4] {'row'}, dimensions={0}, use_global_device_ids=true | all-gather | bytes 4608 | tf_op jit(solution)/shard_map/all_gather | solution.py:58
  168.0 0.1 dynamic_slice.45
  168.1 0.2 fusion.25
  168.3 5.7 %psum.36 = f32[256]{0:T(256)S(1)} all-reduce(f32[256]{0:T(256)S(1)} %bitcast.176), channel_id=1, replica_groups=mesh['row'=8,'col'=4] {'col'}, use_global_device_ids=true, to_apply=%region_3.4 | all-reduce | flops 256 | bytes 2048 | tf_op jit(solution)/shard_map/psum | solution.py:42
  174.0 0.1 copy.32
  174.1 18.3 %all-gather.5 = bf16[8,1,256]{2,1,0:T(2,128)(2,1)S(1)} all-gather(bf16[1,1,256]{2,1,0:T(2,128)(2,1)S(1)} %reshape.50), channel_id=1, replica_groups=mesh['row'=8,'col'=4] {'row'}, dimensions={0}, use_global_device_ids=true | all-gather | bytes 4608 | tf_op jit(solution)/shard_map/all_gather | solution.py:47
  192.4 0.9 fusion.34
  193.4 31.7 %all_gather.38 = bf16[2048,128]{0,1:T(8,128)(2,1)S(1)} all-gather(bf16[256,128]{0,1:T(8,128)(2,1)S(1)} %fusion.34), channel_id=1, replica_groups=mesh['row'=8,'col'=4] {'row'}, dimensions={0}, use_global_device_ids=true | all-gather | bytes 589824 | tf_op jit(solution)/shard_map/all_gather | solution.py:46
  225.1 1.7 convolution_convert_fusion.1
  226.8 31.3 %all_gather.39 = bf16[2048,128]{0,1:T(8,128)(2,1)S(1)} all-gather(bf16[256,128]{0,1:T(8,128)(2,1)S(1)} %bitcast.164), channel_id=1, replica_groups=mesh['row'=8,'col'=4] {'row'}, dimensions={0}, use_global_device_ids=true | all-gather | bytes 589824 | tf_op jit(solution)/shard_map/all_gather | solution.py:57
  258.1 0.8 copy.46
  258.9 3.6 all-to-all-start.1
  262.5 1.6 fusion.9
  264.1 16.5 %all-gather.6 = bf16[8,1,256]{2,1,0:T(2,128)(2,1)S(1)} all-gather(bf16[1,1,256]{2,1,0:T(2,128)(2,1)S(1)} %reshape.52), channel_id=1, replica_groups=mesh['row'=8,'col'=4] {'row'}, dimensions={0}, use_global_device_ids=true | all-gather | bytes 4608 | tf_op jit(solution)/shard_map/all_gather | solution.py:58
  280.6 0.1 dynamic_slice.46
  280.7 0.1 copy.27
  280.9 0.1 copy.33
  281.0 0.1 convolution_bitcast_fusion.6
  281.1 0.1 convolution_bitcast_fusion.5
  281.3 1.3 convolution_bitcast_fusion
  282.6 0.6 pad_maximum_fusion.1
  283.2 0.1 fusion.3
  283.3 0.3 fusion.53
  283.6 0.3 fusion.40
  283.9 0.3 convolution_add_fusion.3
  284.2 19.5 %reduce-scatter.6.cloned.1.call-done = f32[256,128]{0,1:T(8,128)} async-done(((f32[256,512]{0,1:T(8,128)}), f32[256,128]{0,1:T(8,128)}) %reduce-scatter.6.cloned.1.call-update) | async-done | bytes 131088 | tf_op jit(solution)/shard_map/reduce_scatter | solution.py:41
  303.7 0.9 fusion.33
  304.6 31.5 %all_gather.40 = bf16[2048,128]{0,1:T(8,128)(2,1)S(1)} all-gather(bf16[256,128]{0,1:T(8,128)(2,1)S(1)} %fusion.33), channel_id=1, replica_groups=mesh['row'=8,'col'=4] {'row'}, dimensions={0}, use_global_device_ids=true | all-gather | bytes 589824 | tf_op jit(solution)/shard_map/all_gather | solution.py:46
  336.0 1.7 convolution_convert_fusion
  337.8 31.2 %all_gather.46 = bf16[2048,128]{0,1:T(8,128)(2,1)S(1)} all-gather(bf16[256,128]{0,1:T(8,128)(2,1)S(1)} %bitcast.166), channel_id=1, replica_groups=mesh['row'=8,'col'=4] {'row'}, dimensions={0}, use_global_device_ids=true | all-gather | bytes 589824 | tf_op jit(solution)/shard_map/all_gather | solution.py:57
  368.9 0.8 copy.45
  369.8 3.5 all-to-all-start.2
  373.3 0.1 convolution_bitcast_fusion.3
  373.4 0.3 convolution_add_fusion.1
  373.8 0.8 copy.29
  374.6 7.4 %all-to-all-done.2 = bf16[4,512,128]{1,2,0:T(8,128)(2,1)S(1)} async-done(((bf16[4,512,128]{1,2,0:T(8,128)(2,1)}), bf16[4,512,128]{1,2,0:T(8,128)(2,1)S(1)}, u32[]{:S(2)}, u32[]{:S(2)}) %all-to-all-start.2) | async-done | bytes 524320 | tf_op jit(solution)/shard_map/all_to_all | solution.py:60
  382.0 0.1 convolution_bitcast_fusion.2
  382.2 0.9 fusion.1
  383.1 0.9 convolution_add_fusion.2
  384.1 0.1 fusion.5
  384.2 5.7 %all-reduce = (f32[128]{0:T(128)S(1)}, f32[64]{0:T(128)S(1)}) all-reduce(f32[128]{0:T(128)S(1)} %fusion.3, f32[64]{0:T(128)S(1)} %fusion.5), channel_id=1, replica_groups=mesh['row'=8,'col'=4] {'col'}, use_global_device_ids=true, to_apply=%region_5.6 | all-reduce | flops 192 | bytes 1536 | tf_op jit(solution)/shard_map/psum | solution.py:80
  390.0 0.5 broadcast_multiply_fusion.1
  390.5 0.5 sub.23
  391.0 25.1 %all-reduce.3.cloned.1.call-done = f32[64,512]{1,0:T(8,128)} async-done(((f32[64,512]{1,0:T(8,128)}), f32[64,512]{1,0:T(8,128)}) %all-reduce.3.cloned.1.call-update) | async-done | bytes 131088 | tf_op jit(solution)/shard_map/psum | solution.py:80
  416.1 1.6 broadcast_multiply_fusion
  417.7 20.4 %reduce-scatter.8.cloned.1.call-done = bf16[128,128]{0,1:T(8,128)(2,1)} async-done(((bf16[128,512]{0,1:T(8,128)(2,1)}), bf16[128,128]{0,1:T(8,128)(2,1)}) %reduce-scatter.8.cloned.1.call-update) | async-done | bytes 32784 | tf_op jit(solution)/shard_map/reduce_scatter | solution.py:76
  438.0 0.8 convert_subtract_fusion.2
  438.8 0.7 copy.30
  (49 shorter events, 0.5 us)
Async XLA Ops:
  7.2 78.6 %copy-start.3 = (f32[3,256]{1,0:T(4,128)S(1)}, f32[3,256]{1,0:T(4,128)}, u32[]{:S(2)}) copy-start(f32[3,256]{1,0:T(4,128)} %param.9) | copy-start | bytes 9220
  15.3 109.4 %copy-start = (bf16[3,256,512]{2,1,0:T(8,128)(2,1)S(1)}, bf16[3,256,512]{2,1,0:T(8,128)(2,1)}, u32[]{:S(2)}) copy-start(bf16[3,256,512]{2,1,0:T(8,128)(2,1)} %param.12) | copy-start | bytes 2359300
  82.3 48.3 %all-to-all-start = ((bf16[4,512,128]{1,2,0:T(8,128)(2,1)}), bf16[4,512,128]{1,2,0:T(8,128)(2,1)S(1)}, u32[]{:S(2)}, u32[]{:S(2)}) async-start(bf16[4,512,128]{1,2,0:T(8,128)(2,1)} %bitcast.146), calls=%async_computation | async-start | bytes 1048576 | tf_op jit(solution)/shard_map/all_to_all | solution.py:60
  85.7 106.7 %reduce-scatter.4.cloned.1.call-start = ((), (), s32[]{:S(2)}) async-start(), calls=%async_computation.6 | async-start | bytes 655360 | tf_op jit(solution)/shard_map/reduce_scatter | solution.py:41
  193.3 87.4 %copy-start.2 = (bf16[128,128]{1,0:T(8,128)(2,1)S(1)}, bf16[128,128]{1,0:T(8,128)(2,1)}, u32[]{:S(2)}) copy-start(bf16[128,128]{1,0:T(8,128)(2,1)} %param.14) | copy-start | bytes 98308
  193.4 87.6 %copy-start.1 = (bf16[128,3,512]{2,0,1:T(8,128)(2,1)S(1)}, bf16[128,3,512]{2,0,1:T(8,128)(2,1)}, u32[]{:S(2)}) copy-start(bf16[128,3,512]{2,0,1:T(8,128)(2,1)} %param.13) | copy-start | bytes 1179652
  258.9 22.4 %all-to-all-start.1 = ((bf16[4,512,128]{1,2,0:T(8,128)(2,1)}), bf16[4,512,128]{1,2,0:T(8,128)(2,1)S(1)}, u32[]{:S(2)}, u32[]{:S(2)}) async-start(bf16[4,512,128]{1,2,0:T(8,128)(2,1)} %bitcast.145), calls=%async_computation.2 | async-start | bytes 1048576 | tf_op jit(solution)/shard_map/all_to_all | solution.py:60
  262.5 41.2 %reduce-scatter.6.cloned.1.call-start = ((), (), s32[]{:S(2)}) async-start(), calls=%async_computation.7 | async-start | bytes 655360 | tf_op jit(solution)/shard_map/reduce_scatter | solution.py:41
  368.9 21.6 %copy-start.4 = (f32[128]{0:T(128)S(1)}, f32[128]{0:T(128)}, u32[]{:S(2)}) copy-start(f32[128]{0:T(128)} %param.15) | copy-start | bytes 1540
  369.8 12.3 %all-to-all-start.2 = ((bf16[4,512,128]{1,2,0:T(8,128)(2,1)}), bf16[4,512,128]{1,2,0:T(8,128)(2,1)S(1)}, u32[]{:S(2)}, u32[]{:S(2)}) async-start(bf16[4,512,128]{1,2,0:T(8,128)(2,1)} %bitcast.144), calls=%async_computation.4 | async-start | bytes 1048576 | tf_op jit(solution)/shard_map/all_to_all | solution.py:60
  373.3 42.8 %all-reduce.3.cloned.1.call-start = ((), (), s32[]{:S(2)}) async-start(), calls=%async_computation.9 | async-start | bytes 262144 | tf_op jit(solution)/shard_map/psum | solution.py:80
  384.1 54.0 %reduce-scatter.8.cloned.1.call-start = ((), (), s32[]{:S(2)}) async-start(), calls=%async_computation.8 | async-start | bytes 163840 | tf_op jit(solution)/shard_map/reduce_scatter | solution.py:76
Sparse Core Ops, SparseCore 0:
  131.8 20.9 reduce-scatter.3
  282.7 20.9 reduce-scatter.5
  384.2 31.8 all-reduce.2
  418.4 19.6 reduce-scatter.7
where the time goes:
time: 447 us; the launch traced here: 446 us
  blocking collectives  314 us (70%)
  waiting for transfers between devices  72.4 us (16%)
  between operations  19.8 us (4%)
  matrix products  16.5 us (4%)
  starting transfers between devices  10.6 us (2%)
  local copies, waits for them, and re-layouts  7.06 us (2%)
  other arithmetic  5.95 us (1%)
    all_gather x3, blocking collectives, shards(): lax.all_gather(residual, 'row', axis=0, tiled=True)  96.4 us
    all_gather x3, blocking collectives, shards(): lax.all_gather(tile, 'row', axis=0, tiled=True)  93.7 us
    all_gather x3, blocking collectives, shards(): lax.all_gather(resid_resp, 'row', axis=0, tiled=True)  57.4 us
    all_gather x3, blocking collectives, shards(): lax.all_gather(tile_resp, 'row', axis=0, tiled=True)  49.1 us
    psum x1, waiting for transfers between devices, shards(): gram, right, resp_sum = lax.psum((gram, right, trail_resp_total), 'col')  25.1 us
    reduce_scatter x1, waiting for transfers between devices, shards(): lax.psum_scatter(trail_total.astype(jnp.bfloat16), 'col', scatter_dimensi...  20.4 us
    reduce_scatter x2, waiting for transfers between devices, shards(): lax.psum_scatter(update, 'col', scatter_dimension=1, tiled=True)  19.5 us
    psum x2, blocking collectives, shards(): pending_resp = pending_resp - lax.psum(update_resp, 'col')  11.3 us
  transfers between devices with their start and end apart: 7, of which 4 were waited for; matrix products, arithmetic and copies ran while one was open for 3% of the time, Pallas kernels for 0%

commit v1 on v0

--- a/solution.py
+++ b/solution.py
@@ -2,6 +2,18 @@
 import jax.numpy as jnp
 from jax import lax
 from jax.sharding import PartitionSpec as P
+
+
+def doubled_up(value, axis, dim):
+    ways, here, hop = (lax.axis_size(axis), lax.axis_index(axis), value.shape[dim])
+    line, have = (value, 1)
+    while have < ways:
+        line = jnp.concatenate(
+            [line, lax.ppermute(line, axis, [(d, (d - have) % ways) for d in range(ways)])],
+            axis=dim,
+        )
+        have = 2 * have
+    return jnp.roll(line, here * hop, axis=dim)
 
 
 def shards(
@@ -54,7 +66,7 @@
         out_tiles.append(tile)
         out_resp.append(tile_resp)
         all_rows, all_resp = (
-            lax.all_gather(tile, "row", axis=0, tiled=True),
+            doubled_up(tile, "row", 0),
             lax.all_gather(tile_resp, "row", axis=0, tiled=True),
         )
         mine = lax.all_to_all(all_rows, "col", split_axis=0, concat_axis=1, tiled=True)

time: 447 us -> 410 us (0.917)
  blocking collectives: 314 us -> 229 us
  waiting for transfers between devices: 72.4 us -> 110 us
  starting transfers between devices: 10.6 us -> 19 us
    all_gather x3 -> x0, blocking collectives: 93.7 us -> none  [shards(): lax.all_gather(tile, 'row', axis=0, tiled=True)]
    ppermute x0 -> x9, waiting for transfers between devices: none -> 35.9 us  [doubled_up(): lax.ppermute(line, axis, [(d, (d - have) % ways) for d in range(ways)])]
    ppermute x0 -> x9, starting transfers between devices: none -> 11.8 us  [doubled_up(): lax.ppermute(line, axis, [(d, (d - have) % ways) for d in range(ways)])]
    all_to_all x0 -> x1, blocking collectives: none -> 11.4 us  [shards(): lax.all_to_all(all_rows, 'col', split_axis=0, concat_axis=1, tiled=True)]
    all_gather x3, blocking collectives: 57.4 us -> 52 us  [shards(): lax.all_gather(resid_resp, 'row', axis=0, tiled=True)]
    all_to_all x3 -> x2, starting transfers between devices: 10.5 us -> 7.08 us  [shards(): lax.all_to_all(all_rows, 'col', split_axis=0, concat_axis=1, tiled=True)]
  transfers between devices with their start and end apart: 7 -> 15, of which waited for: 4 -> 11; matrix products, arithmetic and copies ran while one was open for 3% -> 3% of each run, Pallas kernels for 0% -> 0%
where the time goes in v1:
time: 410 us
  blocking collectives  229 us (56%)
  waiting for transfers between devices  110 us (27%)
  between operations  19.9 us (5%)
  starting transfers between devices  19 us (5%)
  matrix products  16.6 us (4%)
  other arithmetic  7.89 us (2%)
  local copies, waits for them, and re-layouts  7.5 us (2%)
    all_gather x3, blocking collectives, shards(): lax.all_gather(residual, 'row', axis=0, tiled=True)  95.9 us
    all_gather x3, blocking collectives, shards(): lax.all_gather(tile_resp, 'row', axis=0, tiled=True)  52.1 us
    all_gather x3, blocking collectives, shards(): lax.all_gather(resid_resp, 'row', axis=0, tiled=True)  52 us
    ppermute x9, waiting for transfers between devices, doubled_up(): lax.ppermute(line, axis, [(d, (d - have) % ways) for d in range(ways)])  35.9 us
    psum x1, waiting for transfers between devices, shards(): gram, right, resp_sum = lax.psum((gram, right, trail_resp_total), 'col')  25 us
    reduce_scatter x2, waiting for transfers between devices, shards(): lax.psum_scatter(update, 'col', scatter_dimension=1, tiled=True)  20.9 us
    reduce_scatter x1, waiting for transfers between devices, shards(): lax.psum_scatter(trail_total.astype(jnp.bfloat16), 'col', scatter_dimensi...  20.4 us
    ppermute x9, starting transfers between devices, doubled_up(): lax.ppermute(line, axis, [(d, (d - have) % ways) for d in range(ways)])  11.8 us
  transfers between devices with their start and end apart: 15, of which 11 were waited for; matrix products, arithmetic and copies ran while one was open for 3% of the time, Pallas kernels for 0%

profile of v1, /device:TPU:0, one launch (start us, length us, event | category | flops | bytes accessed | tf_op | source)
XLA Modules:
  0.0 409.5 jit_solution(16997572274488350236)
XLA Ops:
  7.2 1.4 fusion.86
  14.4 0.9 constant_dynamic-slice_fusion.3
  15.3 33.0 %all-gather = bf16[1,2048,128]{2,1,0:T(8,128)(2,1)S(1)} all-gather(bf16[1,256,128]{2,1,0:T(8,128)(2,1)S(1)} %get-tuple-element.35), channel_id=2, replica_groups=mesh['row'=8,'col'=4] {'row'}, dimensions={1}, use_global_device_ids=true | all-gather | bytes 589824 | tf_op jit(solution)/shard_map/all_gather | solution.py:58
  48.4 1.8 convolution_convert_fusion.2
  50.2 4.4 %collective-permute-start = (bf16[256,128]{0,1:T(8,128)(2,1)S(1)}, bf16[256,128]{0,1:T(8,128)(2,1)S(1)}, u32[]{:S(2)}, u32[]{:S(2)}) collective-permute-start(bf16[256,128]{0,1:T(8,128)(2,1)S(1)} %bitcast.149), channel_id=1, source_target_pairs={{0,28},{4,0},{8,4},{12,8},{16,12},{20,16},{24,20},{28,24},{1,29},{... | collective-permute-start | bytes 196616 | tf_op jit(solution)/shard_map/ppermute | solution.py:12
  54.6 2.5 collective-permute-done
  57.1 0.4 collective-permute-start.1
  57.4 6.9 %collective-permute-done.1 = bf16[512,128]{0,1:T(8,128)(2,1)S(1)} collective-permute-done((bf16[512,128]{0,1:T(8,128)(2,1)S(1)}, bf16[512,128]{0,1:T(8,128)(2,1)S(1)}, u32[]{:S(2)}, u32[]{:S(2)}) %collective-permute-start.1) | collective-permute-done | bytes 131104 | tf_op jit(solution)/shard_map/ppermute | solution.py:12
  64.5 9.1 %collective-permute-done.2 = bf16[1024,128]{0,1:T(8,128)(2,1)S(1)} collective-permute-done((bf16[1024,128]{0,1:T(8,128)(2,1)S(1)}, bf16[1024,128]{0,1:T(8,128)(2,1)S(1)}, u32[]{:S(2)}, u32[]{:S(2)}) %collective-permute-start.2) | collective-permute-done | bytes 262176 | tf_op jit(solution)/shard_map/ppermute | solution.py:12
  73.5 0.6 fusion.41
  74.1 0.3 copy.34
  74.4 11.4 %all_to_all.54 = bf16[4,512,128]{2,1,0:T(8,128)(2,1)S(1)} all-to-all(bf16[4,512,128]{2,1,0:T(8,128)(2,1)S(1)} %bitcast.147), channel_id=1, replica_groups=mesh['row'=8,'col'=4] {'col'}, dimensions={0} | all-to-all | bytes 1048576 | tf_op jit(solution)/shard_map/all_to_all | solution.py:72
  86.1 1.1 convolution_bitcast_fusion.1
  87.3 20.9 %reduce-scatter.4.cloned.1.call-done = f32[256,128]{0,1:T(8,128)} async-done(((f32[256,512]{0,1:T(8,128)}), f32[256,128]{0,1:T(8,128)}) %reduce-scatter.4.cloned.1.call-update) | async-done | bytes 131088 | tf_op jit(solution)/shard_map/reduce_scatter | solution.py:53
  108.2 0.9 fusion.55
  109.2 31.5 %all_gather.28 = bf16[2048,128]{0,1:T(8,128)(2,1)S(1)} all-gather(bf16[256,128]{0,1:T(8,128)(2,1)S(1)} %fusion.55), channel_id=1, replica_groups=mesh['row'=8,'col'=4] {'row'}, dimensions={0}, use_global_device_ids=true | all-gather | bytes 589824 | tf_op jit(solution)/shard_map/all_gather | solution.py:58
  140.7 1.7 convolution_convert_fusion.1
  142.4 4.3 %collective-permute-start.3 = (bf16[256,128]{0,1:T(8,128)(2,1)S(1)}, bf16[256,128]{0,1:T(8,128)(2,1)S(1)}, u32[]{:S(2)}, u32[]{:S(2)}) collective-permute-start(bf16[256,128]{0,1:T(8,128)(2,1)S(1)} %bitcast.154), channel_id=1, source_target_pairs={{0,28},{4,0},{8,4},{12,8},{16,12},{20,16},{24,20},{28,24},{1,29},{... | collective-permute-start | bytes 196616 | tf_op jit(solution)/shard_map/ppermute | solution.py:12
  146.7 16.4 %all-gather.1 = bf16[1,2048]{1,0:T(2,128)(2,1)S(1)} all-gather(bf16[1,256]{1,0:T(2,128)(2,1)S(1)} %fusion.84), channel_id=3, replica_groups=mesh['row'=8,'col'=4] {'row'}, dimensions={1}, use_global_device_ids=true | all-gather | bytes 4608 | tf_op jit(solution)/shard_map/all_gather | solution.py:59
  163.1 0.3 collective-permute-start.4
  163.4 1.6 fusion.15
  165.0 18.6 %all-gather.2 = bf16[8,1,256]{2,1,0:T(2,128)(2,1)S(1)} all-gather(bf16[1,1,256]{2,1,0:T(2,128)(2,1)S(1)} %reshape.44), channel_id=1, replica_groups=mesh['row'=8,'col'=4] {'row'}, dimensions={0}, use_global_device_ids=true | all-gather | bytes 4608 | tf_op jit(solution)/shard_map/all_gather | solution.py:70
  184.0 6.0 %psum.35 = f32[256]{0:T(256)S(1)} all-reduce(f32[256]{0:T(256)S(1)} %bitcast.173), channel_id=1, replica_groups=mesh['row'=8,'col'=4] {'col'}, use_global_device_ids=true, to_apply=%region_2.4 | all-reduce | flops 256 | bytes 2048 | tf_op jit(solution)/shard_map/psum | solution.py:54
  189.9 2.1 collective-permute-done.5
  192.1 0.6 fusion.34
  192.7 1.0 copy.38
  193.7 3.5 all-to-all-start.1
  197.3 17.8 %all-gather.3 = bf16[8,1,256]{2,1,0:T(2,128)(2,1)S(1)} all-gather(bf16[1,1,256]{2,1,0:T(2,128)(2,1)S(1)} %reshape.46), channel_id=1, replica_groups=mesh['row'=8,'col'=4] {'row'}, dimensions={0}, use_global_device_ids=true | all-gather | bytes 4608 | tf_op jit(solution)/shard_map/all_gather | solution.py:59
  215.1 1.6 fusion.12
  216.7 16.8 %all-gather.4 = bf16[8,1,256]{2,1,0:T(2,128)(2,1)S(1)} all-gather(bf16[1,1,256]{2,1,0:T(2,128)(2,1)S(1)} %reshape.48), channel_id=1, replica_groups=mesh['row'=8,'col'=4] {'row'}, dimensions={0}, use_global_device_ids=true | all-gather | bytes 4608 | tf_op jit(solution)/shard_map/all_gather | solution.py:70
  233.9 1.3 convolution_bitcast_fusion
  235.2 0.2 fusion.46
  235.5 5.7 %psum.36 = f32[256]{0:T(256)S(1)} all-reduce(f32[256]{0:T(256)S(1)} %bitcast.172), channel_id=1, replica_groups=mesh['row'=8,'col'=4] {'col'}, use_global_device_ids=true, to_apply=%region_3.5 | all-reduce | flops 256 | bytes 2048 | tf_op jit(solution)/shard_map/psum | solution.py:54
  241.1 17.8 %all-gather.5 = bf16[8,1,256]{2,1,0:T(2,128)(2,1)S(1)} all-gather(bf16[1,1,256]{2,1,0:T(2,128)(2,1)S(1)} %reshape.50), channel_id=1, replica_groups=mesh['row'=8,'col'=4] {'row'}, dimensions={0}, use_global_device_ids=true | all-gather | bytes 4608 | tf_op jit(solution)/shard_map/all_gather | solution.py:59
  259.0 1.6 fusion.9
  260.6 16.8 %all-gather.6 = bf16[8,1,256]{2,1,0:T(2,128)(2,1)S(1)} all-gather(bf16[1,1,256]{2,1,0:T(2,128)(2,1)S(1)} %reshape.52), channel_id=1, replica_groups=mesh['row'=8,'col'=4] {'row'}, dimensions={0}, use_global_device_ids=true | all-gather | bytes 4608 | tf_op jit(solution)/shard_map/all_gather | solution.py:70
  278.2 0.9 fusion.54
  279.1 31.4 %all_gather.29 = bf16[2048,128]{0,1:T(8,128)(2,1)S(1)} all-gather(bf16[256,128]{0,1:T(8,128)(2,1)S(1)} %fusion.54), channel_id=1, replica_groups=mesh['row'=8,'col'=4] {'row'}, dimensions={0}, use_global_device_ids=true | all-gather | bytes 589824 | tf_op jit(solution)/shard_map/all_gather | solution.py:58
  310.5 1.7 convolution_convert_fusion
  312.2 1.6 collective-permute-start.6
  313.8 0.6 pad_maximum_fusion.7
  314.4 2.1 collective-permute-done.6
  316.5 0.6 collective-permute-start.7
  317.1 0.3 fusion.61
  317.4 4.1 %collective-permute-done.7 = bf16[512,128]{0,1:T(8,128)(2,1)S(1)} collective-permute-done((bf16[512,128]{0,1:T(8,128)(2,1)S(1)}, bf16[512,128]{0,1:T(8,128)(2,1)S(1)}, u32[]{:S(2)}, u32[]{:S(2)}) %collective-permute-start.7) | collective-permute-done | bytes 131104 | tf_op jit(solution)/shard_map/ppermute | solution.py:12
  321.7 0.3 fusion.74
  321.9 0.3 convolution_add_fusion.3
  322.2 9.0 %collective-permute-done.8 = bf16[1024,128]{0,1:T(8,128)(2,1)S(1)} collective-permute-done((bf16[1024,128]{0,1:T(8,128)(2,1)S(1)}, bf16[1024,128]{0,1:T(8,128)(2,1)S(1)}, u32[]{:S(2)}, u32[]{:S(2)}) %collective-permute-start.8) | collective-permute-done | bytes 262176 | tf_op jit(solution)/shard_map/ppermute | solution.py:12
  331.3 0.6 fusion.27
  331.9 1.0 copy.42
  332.9 3.6 all-to-all-start.2
  336.7 0.3 convolution_add_fusion.1
  337.0 0.8 copy.44
  337.8 7.5 %all-to-all-done.2 = bf16[4,512,128]{2,1,0:T(8,128)(2,1)S(1)} async-done(((bf16[4,512,128]{2,1,0:T(8,128)(2,1)}), bf16[4,512,128]{2,1,0:T(8,128)(2,1)S(1)}, u32[]{:S(2)}, u32[]{:S(2)}) %all-to-all-start.2) | async-done | bytes 524320 | tf_op jit(solution)/shard_map/all_to_all | solution.py:72
  345.7 1.0 fusion.1
  346.6 0.9 convolution_add_fusion.2
  347.8 5.7 %all-reduce = (f32[128]{0:T(128)S(1)}, f32[64]{0:T(128)S(1)}) all-reduce(f32[128]{0:T(128)S(1)} %fusion.3, f32[64]{0:T(128)S(1)} %fusion.5), channel_id=1, replica_groups=mesh['row'=8,'col'=4] {'col'}, use_global_device_ids=true, to_apply=%region_5.7 | all-reduce | flops 192 | bytes 1536 | tf_op jit(solution)/shard_map/psum | solution.py:92
  353.6 0.5 broadcast_multiply_fusion.1
  354.1 0.5 sub.26
  354.6 25.0 %all-reduce.3.cloned.1.call-done = f32[64,512]{1,0:T(8,128)} async-done(((f32[64,512]{1,0:T(8,128)}), f32[64,512]{1,0:T(8,128)}) %all-reduce.3.cloned.1.call-update) | async-done | bytes 131088 | tf_op jit(solution)/shard_map/psum | solution.py:92
  379.5 1.6 broadcast_multiply_fusion
  381.1 20.4 %reduce-scatter.8.cloned.1.call-done = bf16[128,128]{0,1:T(8,128)(2,1)} async-done(((bf16[128,512]{0,1:T(8,128)(2,1)}), bf16[128,128]{0,1:T(8,128)(2,1)}) %reduce-scatter.8.cloned.1.call-update) | async-done | bytes 32784 | tf_op jit(solution)/shard_map/reduce_scatter | solution.py:88
  401.5 0.8 convert_subtract_fusion.2
  402.2 0.7 copy.45
  (75 shorter events, 3.1 us)
Async XLA Ops:
  7.2 101.1 %reduce-scatter.4.cloned.1.call-start = ((), (), s32[]{:S(2)}) async-start(), calls=%async_computation.6 | async-start | bytes 655360 | tf_op jit(solution)/shard_map/reduce_scatter | solution.py:53
  48.4 37.7 %copy-start = (bf16[3,256,512]{2,1,0:T(8,128)(2,1)S(1)}, bf16[3,256,512]{2,1,0:T(8,128)(2,1)}, u32[]{:S(2)}) copy-start(bf16[3,256,512]{2,1,0:T(8,128)(2,1)} %param.14) | copy-start | bytes 2359300
  50.2 6.9 %collective-permute-start = (bf16[256,128]{0,1:T(8,128)(2,1)S(1)}, bf16[256,128]{0,1:T(8,128)(2,1)S(1)}, u32[]{:S(2)}, u32[]{:S(2)}) collective-permute-start(bf16[256,128]{0,1:T(8,128)(2,1)S(1)} %bitcast.149), channel_id=1, source_target_pairs={{0,28},{4,0},{8,4},{12,8},{16,12},{20,16},{24,20},{28,24},{1,29},{... | collective-permute-start | bytes 196616 | tf_op jit(solution)/shard_map/ppermute | solution.py:12
  57.1 7.3 %collective-permute-start.1 = (bf16[512,128]{0,1:T(8,128)(2,1)S(1)}, bf16[512,128]{0,1:T(8,128)(2,1)S(1)}, u32[]{:S(2)}, u32[]{:S(2)}) collective-permute-start(bf16[512,128]{0,1:T(8,128)(2,1)S(1)} %pad_maximum_fusion.4), channel_id=1, source_target_pairs={{0,24},{4,28},{8,0},{12,4},{16,8},{20,12},{24,16},{28,20},{1,25},{... | collective-permute-start | bytes 393224 | tf_op jit(solution)/shard_map/ppermute | solution.py:12
  64.4 9.2 %collective-permute-start.2 = (bf16[1024,128]{0,1:T(8,128)(2,1)S(1)}, bf16[1024,128]{0,1:T(8,128)(2,1)S(1)}, u32[]{:S(2)}, u32[]{:S(2)}) collective-permute-start(bf16[1024,128]{0,1:T(8,128)(2,1)S(1)} %pad_maximum_fusion), channel_id=1, source_target_pairs={{0,16},{4,20},{8,24},{12,28},{16,0},{20,4},{24,8},{28,12},{1,17},{... | collective-permute-start | bytes 786440 | tf_op jit(solution)/shard_map/ppermute | solution.py:12
  74.4 72.3 %copy-start.3 = (f32[3,256]{1,0:T(4,128)S(1)}, f32[3,256]{1,0:T(4,128)}, u32[]{:S(2)}) copy-start(f32[3,256]{1,0:T(4,128)} %param.11) | copy-start | bytes 9220
  142.4 20.7 %collective-permute-start.3 = (bf16[256,128]{0,1:T(8,128)(2,1)S(1)}, bf16[256,128]{0,1:T(8,128)(2,1)S(1)}, u32[]{:S(2)}, u32[]{:S(2)}) collective-permute-start(bf16[256,128]{0,1:T(8,128)(2,1)S(1)} %bitcast.154), channel_id=1, source_target_pairs={{0,28},{4,0},{8,4},{12,8},{16,12},{20,16},{24,20},{28,24},{1,29},{... | collective-permute-start | bytes 196616 | tf_op jit(solution)/shard_map/ppermute | solution.py:12
  163.1 20.6 %collective-permute-start.4 = (bf16[512,128]{0,1:T(8,128)(2,1)S(1)}, bf16[512,128]{0,1:T(8,128)(2,1)S(1)}, u32[]{:S(2)}, u32[]{:S(2)}) collective-permute-start(bf16[512,128]{0,1:T(8,128)(2,1)S(1)} %pad_maximum_fusion.5), channel_id=1, source_target_pairs={{0,24},{4,28},{8,0},{12,4},{16,8},{20,12},{24,16},{28,20},{1,25},{... | collective-permute-start | bytes 393224 | tf_op jit(solution)/shard_map/ppermute | solution.py:12
  183.7 8.3 %collective-permute-start.5 = (bf16[1024,128]{0,1:T(8,128)(2,1)S(1)}, bf16[1024,128]{0,1:T(8,128)(2,1)S(1)}, u32[]{:S(2)}, u32[]{:S(2)}) collective-permute-start(bf16[1024,128]{0,1:T(8,128)(2,1)S(1)} %pad_maximum_fusion.1), channel_id=1, source_target_pairs={{0,16},{4,20},{8,24},{12,28},{16,0},{20,4},{24,8},{28,12},{1,17},{... | collective-permute-start | bytes 786440 | tf_op jit(solution)/shard_map/ppermute | solution.py:12
  193.7 39.9 %all-to-all-start.1 = ((bf16[4,512,128]{2,1,0:T(8,128)(2,1)}), bf16[4,512,128]{2,1,0:T(8,128)(2,1)S(1)}, u32[]{:S(2)}, u32[]{:S(2)}) async-start(bf16[4,512,128]{2,1,0:T(8,128)(2,1)} %bitcast.18), calls=%async_computation.2 | async-start | bytes 1048576 | tf_op jit(solution)/shard_map/all_to_all | solution.py:72
  197.2 81.0 %reduce-scatter.6.cloned.1.call-start = ((), (), s32[]{:S(2)}) async-start(), calls=%async_computation.7 | async-start | bytes 655360 | tf_op jit(solution)/shard_map/reduce_scatter | solution.py:53
  233.6 43.9 %copy-start.2 = (bf16[128,128]{1,0:T(8,128)(2,1)S(1)}, bf16[128,128]{1,0:T(8,128)(2,1)}, u32[]{:S(2)}) copy-start(bf16[128,128]{1,0:T(8,128)(2,1)} %param.16) | copy-start | bytes 98308
  233.6 44.1 %copy-start.1 = (bf16[128,3,512]{2,0,1:T(8,128)(2,1)S(1)}, bf16[128,3,512]{2,0,1:T(8,128)(2,1)}, u32[]{:S(2)}) copy-start(bf16[128,3,512]{2,0,1:T(8,128)(2,1)} %param.15) | copy-start | bytes 1179652
  312.2 4.3 %collective-permute-start.6 = (bf16[256,128]{0,1:T(8,128)(2,1)S(1)}, bf16[256,128]{0,1:T(8,128)(2,1)S(1)}, u32[]{:S(2)}, u32[]{:S(2)}) collective-permute-start(bf16[256,128]{0,1:T(8,128)(2,1)S(1)} %bitcast.159), channel_id=1, source_target_pairs={{0,28},{4,0},{8,4},{12,8},{16,12},{20,16},{24,20},{28,24},{1,29},{... | collective-permute-start | bytes 196616 | tf_op jit(solution)/shard_map/ppermute | solution.py:12
  316.5 5.0 %collective-permute-start.7 = (bf16[512,128]{0,1:T(8,128)(2,1)S(1)}, bf16[512,128]{0,1:T(8,128)(2,1)S(1)}, u32[]{:S(2)}, u32[]{:S(2)}) collective-permute-start(bf16[512,128]{0,1:T(8,128)(2,1)S(1)} %pad_maximum_fusion.6), channel_id=1, source_target_pairs={{0,24},{4,28},{8,0},{12,4},{16,8},{20,12},{24,16},{28,20},{1,25},{... | collective-permute-start | bytes 393224 | tf_op jit(solution)/shard_map/ppermute | solution.py:12
  321.6 9.7 %collective-permute-start.8 = (bf16[1024,128]{0,1:T(8,128)(2,1)S(1)}, bf16[1024,128]{0,1:T(8,128)(2,1)S(1)}, u32[]{:S(2)}, u32[]{:S(2)}) collective-permute-start(bf16[1024,128]{0,1:T(8,128)(2,1)S(1)} %pad_maximum_fusion.2), channel_id=1, source_target_pairs={{0,16},{4,20},{8,24},{12,28},{16,0},{20,4},{24,8},{28,12},{1,17},{... | collective-permute-start | bytes 786440 | tf_op jit(solution)/shard_map/ppermute | solution.py:12
  332.9 21.2 %copy-start.4 = (f32[128]{0:T(128)S(1)}, f32[128]{0:T(128)}, u32[]{:S(2)}) copy-start(f32[128]{0:T(128)} %param.17) | copy-start | bytes 1540
  332.9 12.4 %all-to-all-start.2 = ((bf16[4,512,128]{2,1,0:T(8,128)(2,1)}), bf16[4,512,128]{2,1,0:T(8,128)(2,1)S(1)}, u32[]{:S(2)}, u32[]{:S(2)}) async-start(bf16[4,512,128]{2,1,0:T(8,128)(2,1)} %bitcast.37), calls=%async_computation.4 | async-start | bytes 1048576 | tf_op jit(solution)/shard_map/all_to_all | solution.py:72
  336.5 43.0 %all-reduce.3.cloned.1.call-start = ((), (), s32[]{:S(2)}) async-start(), calls=%async_computation.9 | async-start | bytes 262144 | tf_op jit(solution)/shard_map/psum | solution.py:92
  347.6 53.9 %reduce-scatter.8.cloned.1.call-start = ((), (), s32[]{:S(2)}) async-start(), calls=%async_computation.8 | async-start | bytes 163840 | tf_op jit(solution)/shard_map/reduce_scatter | solution.py:88
Sparse Core Ops, SparseCore 0:
  87.3 20.8 reduce-scatter.3
  235.3 20.3 reduce-scatter.5
  347.7 31.7 all-reduce.2
  381.8 19.6 reduce-scatter.7
